TPU v7x, 256 devices: a whole 4x4x8 slice. The times are simulated.
256 devices in a mesh: seq: 8 (over y, core), tensor: 32 (over z, x).
Axes of the slice: x: 4, y: 4, z: 8, core: 2. Of those that a mesh axis runs over, the one named last changes fastest.
Arguments:
- tokens: bfloat16 [4096, 3584], P('seq', 'tensor'), may hold values from -6 to 6
- w_zx: bfloat16 [2, 3584, 4096], P(None, None, 'tensor'), may hold values from -0.09375 to 0.09375
- w_bc: bfloat16 [3584, 128], replicated, may hold values from -0.09375 to 0.09375
- w_dt: bfloat16 [3584, 64], P(None, 'tensor'), may hold values from -0.09375 to 0.09375
- dt_bias: float32 [64], P('tensor'), may hold values from -2 to 0.5
- a_rate: float32 [64], P('tensor'), may hold values from 0.00012207031 to 0.05
- d_skip: float32 [64], P('tensor'), may hold values from 0.3 to 1.5
- conv_x: float32 [4, 4096], P(None, 'tensor'), may hold values from -3 to 3
- conv_bc: float32 [4, 128], replicated, may hold values from -3 to 3
- norm_gain: float32 [4096], P('tensor'), may hold values from 0.25 to 1.75
- w_out: bfloat16 [4096, 3584], P('tensor'), may hold values from -0.09375 to 0.09375
- segments: int32 [4096], P('seq'), may hold values from 0 to 5, never falling along the last dimension, each value on 1 to 2048 neighbouring positions
Outputs:
- mixed: bfloat16 [4096, 3584], P(('seq', 'tensor'))
Inputs may be any that keep to these rules, and one draw needn't show every extreme that they name: `segments`: prompt ids never fall along the tokens, so each prompt's tokens are contiguous.
All inputs are finite; a program needn't handle non-finite values.
Results may differ from a plain program's by a relative error of at most 0.02.
Values may be sent and summed in bfloat16 or wider, within the bound.
A program may use at most 64 MiB of HBM per device.

v0:
```python
import jax
import jax.numpy as jnp
from jax import lax
from jax.sharding import PartitionSpec as P

BLOCK = 256
HIGHEST_PREC = lax.Precision.HIGHEST
NORM_EPS = 1e-05


def from_behind(block, axis, distance):
    devices = range(lax.axis_size(axis))
    route = [(i - distance, i) for i in devices if i - distance in devices]
    return lax.ppermute(block, axis, route)


def entering(array, axis, join, neutral):
    place = lax.axis_index(axis)
    gathered = jax.tree.map(
        lambda a, kind: lax.all_gather(a.astype(kind), axis),
        array,
        jax.tree.map(lambda a: jnp.bfloat16 if a.dtype == jnp.float32 else a.dtype, array),
    )
    state = jax.tree.map(lambda a, e: jnp.zeros_like(a) + jnp.asarray(e, a.dtype), array, neutral)

    def one(turn, state):
        return join(
            state,
            jax.tree.map(
                lambda a, own: lax.dynamic_index_in_dim(a, turn, 0, False).astype(own.dtype),
                gathered,
                array,
            ),
        )

    return lax.fori_loop(0, place, one, state)


def conv_tail(extended, seg_ext, taps, tok_rows):
    conv_len = taps.shape[0]
    seg_now = seg_ext[conv_len - 1 :]
    conv_sum = taps[conv_len - 1] * extended[conv_len - 1 :]
    for offset in range(1, conv_len):
        earlier = extended[conv_len - 1 - offset : conv_len - 1 - offset + tok_rows]
        seg_then = seg_ext[conv_len - 1 - offset : conv_len - 1 - offset + tok_rows]
        conv_sum = conv_sum + taps[conv_len - 1 - offset] * jnp.where(
            (seg_then == seg_now)[:, None], earlier, 0.0
        )
    return jax.nn.silu(conv_sum)


def ssd_block(carry, block):
    state, last_seg = carry
    inner_x, step_size, logdec, bmat, cmat, seg_ids = block
    cum_decay = jnp.cumsum(logdec, axis=0)
    position = jnp.arange(seg_ids.shape[0])
    visible = (seg_ids[:, None] == seg_ids[None, :]) & (position[:, None] >= position[None, :])
    gap_decay = jnp.where(
        visible[:, :, None], cum_decay[:, None, :] - cum_decay[None, :, :], -jnp.inf
    )
    scores = jnp.dot(cmat, bmat.T, precision=HIGHEST_PREC)
    weights = jnp.exp(gap_decay) * scores[:, :, None] * step_size[None, :, :]
    block_out = jnp.einsum("tsh,shp->thp", weights, inner_x, precision=HIGHEST_PREC)
    enter = jnp.where((seg_ids == last_seg)[:, None], jnp.exp(cum_decay), 0.0)
    block_out = block_out + enter[:, :, None] * jnp.einsum(
        "tn,hpn->thp", cmat, state, precision=HIGHEST_PREC
    )
    tail_weight = (
        jnp.where(
            (seg_ids == seg_ids[-1])[:, None], jnp.exp(cum_decay[-1][None, :] - cum_decay), 0.0
        )
        * step_size
    )
    carry_keep = jnp.where(seg_ids[-1] == last_seg, jnp.exp(cum_decay[-1]), 0.0)
    new_state = carry_keep[:, None, None] * state + jnp.einsum(
        "sh,shp,sn->hpn", tail_weight, inner_x, bmat, precision=HIGHEST_PREC
    )
    return ((new_state, seg_ids[-1]), block_out)


def link_states(earlier, later):
    gain_a, state_a, first_a, last_a = earlier
    gain_b, state_b, first_b, last_b = later
    joined = (first_b == last_a) | (last_a < 0.0) | (first_b < 0.0)
    passing = jnp.where(joined, gain_b, 0.0)
    merged_gain = gain_a * passing
    merged_state = passing[:, None, None] * state_a + state_b
    merged_first = jnp.where(first_a < 0.0, first_b, first_a)
    merged_last = jnp.where(last_b < 0.0, last_a, last_b)
    return (merged_gain, merged_state, merged_first, merged_last)


def local(
    tokens, w_zx, w_bc, w_dt, dt_bias, a_rate, d_skip, conv_x, conv_bc, norm_gain, w_out, segments
):
    tok_rows = tokens.shape[0]
    inner_w = w_zx.shape[2]
    heads = dt_bias.shape[0]
    head_size = inner_w // heads
    state_w = w_bc.shape[1] // 2
    rim_len = conv_x.shape[0] - 1
    piece = lax.all_gather(tokens, "tensor", axis=1, tiled=True)
    gate_rows = w_zx[0]
    inner_rows = w_zx[1]
    gate_sum = jnp.dot(piece, gate_rows, preferred_element_type=jnp.float32)
    inner_sum = jnp.dot(piece, inner_rows, preferred_element_type=jnp.float32)
    bc_sum = jnp.dot(piece, w_bc, preferred_element_type=jnp.float32)
    dt_raw = jnp.dot(piece, w_dt, preferred_element_type=jnp.float32)
    gate_proj = gate_sum.astype(jnp.bfloat16)
    inner_proj = inner_sum.astype(jnp.bfloat16)
    bc_proj = bc_sum.astype(jnp.bfloat16)
    rim_inner, rim_bc, rim_seg = from_behind(
        (
            inner_proj[tok_rows - rim_len :],
            bc_proj[tok_rows - rim_len :],
            segments[tok_rows - rim_len :].astype(jnp.bfloat16),
        ),
        "seq",
        1,
    )
    seg_ext = jnp.concatenate([rim_seg.astype(jnp.int32), segments], 0)
    conv_inner = conv_tail(
        jnp.concatenate([rim_inner.astype(jnp.float32), inner_proj.astype(jnp.float32)], 0),
        seg_ext,
        conv_x,
        tok_rows,
    )
    conv_state = conv_tail(
        jnp.concatenate([rim_bc.astype(jnp.float32), bc_proj.astype(jnp.float32)], 0),
        seg_ext,
        conv_bc,
        tok_rows,
    )
    bmat = conv_state[:, :state_w]
    cmat = conv_state[:, state_w:]
    step_size = jax.nn.softplus(dt_raw + dt_bias)
    logdec = -a_rate * step_size
    inner_heads = conv_inner.reshape(tok_rows, heads, head_size)
    nblocks = tok_rows // BLOCK
    blocks = (
        inner_heads.reshape(nblocks, BLOCK, heads, head_size),
        step_size.reshape(nblocks, BLOCK, heads),
        logdec.reshape(nblocks, BLOCK, heads),
        bmat.reshape(nblocks, BLOCK, state_w),
        cmat.reshape(nblocks, BLOCK, state_w),
        segments.reshape(nblocks, BLOCK),
    )
    start_carry = (jnp.zeros((heads, head_size, state_w), jnp.float32), jnp.array(-1, jnp.int32))
    (local_state, _), block_outs = lax.scan(ssd_block, start_carry, blocks)
    cum_device = jnp.cumsum(logdec, axis=0)
    device_gain = jnp.where(segments[0] == segments[-1], jnp.exp(cum_device[-1]), 0.0)
    seg_float = segments.astype(jnp.float32)
    element = (device_gain, local_state, seg_float[:1], seg_float[-1:])
    identity = (
        jnp.ones((heads,), jnp.float32),
        jnp.zeros_like(local_state),
        jnp.full((1,), -1.0, jnp.float32),
        jnp.full((1,), -1.0, jnp.float32),
    )
    incoming = entering(element, "seq", link_states, identity)
    state_in = incoming[1]
    last_in = incoming[3]
    enter = jnp.where((seg_float == last_in[0])[:, None], jnp.exp(cum_device), 0.0)
    ssd_out = block_outs.reshape(tok_rows, heads, head_size)
    ssd_out = ssd_out + enter[:, :, None] * jnp.einsum(
        "tn,hpn->thp", cmat, state_in, precision=HIGHEST_PREC
    )
    ssd_out = ssd_out + d_skip[None, :, None] * inner_heads
    gated = ssd_out.reshape(tok_rows, inner_w) * jax.nn.silu(gate_proj.astype(jnp.float32))
    local_squares = jnp.sum(gated * gated, axis=1)
    total_squares = lax.psum(local_squares, "tensor")
    scale = lax.rsqrt(total_squares / (inner_w * lax.axis_size("tensor")) + NORM_EPS)
    normed = (gated * scale[:, None] * norm_gain).astype(jnp.bfloat16)
    return lax.psum_scatter(
        jnp.dot(normed, w_out, preferred_element_type=jnp.float32).astype(jnp.bfloat16),
        "tensor",
        scatter_dimension=0,
        tiled=True,
    )


def solution(mesh):
    in_specs = (
        P("seq", "tensor"),
        P(None, None, "tensor"),
        P(),
        P(None, "tensor"),
        P("tensor"),
        P("tensor"),
        P("tensor"),
        P(None, "tensor"),
        P(),
        P("tensor"),
        P("tensor", None),
        P("seq"),
    )
    out_specs = P(("seq", "tensor"), None)
    return jax.shard_map(local, mesh=mesh, in_specs=in_specs, out_specs=out_specs, check_vma=False)
```

profile of v0, /device:TPU:8, one launch (start us, length us, event | category | flops | bytes accessed | tf_op | source)
XLA Modules:
  0.0 471.1 jit_solution(9409055045789982205)
XLA Ops:
  6.5 0.7 all-gather.6.cloned.1.call-update
  7.3 0.8 convert_convert_fusion
  8.2 1.3 dynamic-slice
  10.0 1.4 dynamic-update-slice
  11.4 1.3 dynamic-update-slice.1
  12.7 1.9 collective-permute-start
  14.6 12.0 %all-reduce.2 = (bf16[8]{0:T(256)(128)(2,1)S(1)}, bf16[8]{0:T(256)(128)(2,1)S(1)}) all-reduce(bf16[8]{0:T(256)(128)(2,1)S(1)} %dynamic-update-slice, bf16[8]{0:T(256)(128)(2,1)S(1)} %dynamic-update-slice.1), channel_id=2, replica_groups=mesh['seq'=8,'tensor'=32] {'seq'}, use_global_device_ids=true, to_apply=%add | all-reduce | flops 16 | bytes 64
  26.6 0.7 reshape.139
  27.3 0.7 neg.20
  28.0 1.4 fusion.81
  30.7 0.8 slice_bitcast_fusion.8
  31.6 0.8 slice_bitcast_fusion.4
  32.4 0.8 pad_add_fusion
  33.2 0.8 slice_compare_fusion.2
  33.9 59.5 %all-gather.6.cloned.1.call-done = bf16[512,3584]{0,1:T(8,128)(2,1)} async-done(((bf16[512,112]{0,1:T(8,128)(2,1)}), bf16[512,3584]{0,1:T(8,128)(2,1)}) %all-gather.6.cloned.1.call-update) | async-done | bytes 3670032 | tf_op jit(solution)/shard_map/all_gather | solution.py:102
  93.4 2.7 broadcast_multiply_fusion
  96.3 3.6 fusion.83
  99.9 1.9 collective-permute-start.1
  101.8 1.1 fusion.84
  103.0 3.5 collective-permute-start.2
  107.8 8.4 %all-gather.3 = bf16[8,1,2]{2,1,0:T(2,128)(2,1)S(1)} all-gather(bf16[1,1,2]{2,1,0:T(2,128)(2,1)S(1)} %bitcast.197), channel_id=1, replica_groups=mesh['seq'=8,'tensor'=32] {'seq'}, dimensions={0}, use_global_device_ids=true | all-gather | bytes 36 | tf_op jit(solution)/shard_map/all_gather | solution.py:20
  118.0 16.2 %while.31 = (s32[]{:T(128)}, f32[2,64,64]{2,1,0:T(8,128)S(1)}, s32[]{:T(128)}, f32[2,256,2,64]{1,0,3,2:T(2,128)S(1)}, s32[2,256]{1,0:T(2,128)S(1)}, /*index=5*/f...) while((s32[]{:T(128)}, f32[2,64,64]{2,1,0:T(8,128)S(1)}, ...), condition=%wide.region_3.4_spmd.clone, body=%wide.region_0.3_spmd.clone.sunk | while | flops 202246672 | bytes 2326889 | solution.py:149
  122.6 0.8 fusion.114
  123.6 1.9 dynamic_update_slice.6
  130.7 0.8 fusion.114
  131.6 1.9 dynamic_update_slice.6
  134.4 11.6 %all-gather.1 = bf16[16,64,64]{2,1,0:T(8,128)(2,1)S(1)} all-gather(bf16[2,64,64]{2,1,0:T(8,128)(2,1)S(1)} %convert_element_type.85), channel_id=3, replica_groups=mesh['seq'=8,'tensor'=32] {'seq'}, dimensions={0}, use_global_device_ids=true | all-gather | bytes 147456 | tf_op jit(solution)/shard_map/all_gather | solution.py:20
  146.0 6.9 %while.30 = (s32[]{:T(128)}, f32[2,64,64]{2,1,0:T(8,128)S(1)}, f32[1]{0:T(128)}, s32[]{:T(128)}, bf16[8,1]{0,1:T(2,128)(2,1)S(1)}, /*index=5*/bf16[8,2]{0,1:T(2,...) while((s32[]{:T(128)}, f32[2,64,64]{2,1,0:T(8,128)S(1)}, ...), condition=%wide.region_7.8_spmd, body=%wide.region_6.7_spmd.sunk | while | flops 24592 | bytes 82183 | solution.py:36
  153.6 3.5 multiply_reduce_fusion
  157.1 71.9 %psum.7 = f32[512]{0:T(512)S(1)} all-reduce(f32[512]{0:T(512)S(1)} %get-tuple-element.290), channel_id=1, replica_groups=mesh['seq'=8,'tensor'=32] {'tensor'}, use_global_device_ids=true, to_apply=%region_9.10 | all-reduce | flops 512 | bytes 4096 | tf_op jit(solution)/shard_map/psum | solution.py:171
  229.1 3.0 convolution_convert_fusion
  232.1 232.2 %reduce-scatter.2.cloned.1.call-done = bf16[16,3584]{1,0:T(8,128)(2,1)} async-done(((bf16[512,3584]{1,0:T(8,128)(2,1)}), bf16[16,3584]{1,0:T(8,128)(2,1)}) %reduce-scatter.2.cloned.1.call-update) | async-done | bytes 114704 | tf_op jit(solution)/shard_map/reduce_scatter | solution.py:174
  (109 shorter events, 14.7 us)
Async XLA Ops:
  6.5 222.5 %copy-start = (bf16[128,3584]{1,0:T(8,128)(2,1)S(1)}, bf16[128,3584]{1,0:T(8,128)(2,1)}, u32[]{:S(2)}) copy-start(bf16[128,3584]{1,0:T(8,128)(2,1)} %param.26) | copy-start | bytes 2752516
  6.5 86.9 %all-gather.6.cloned.1.call-start = ((), (), s32[]{:S(2)}) async-start(), calls=%async_computation.1 | async-start | bytes 3784704 | tf_op jit(solution)/shard_map/all_gather | solution.py:102
  7.3 457.0 %reduce-scatter.2.cloned.1.call-start = ((), (), s32[]{:S(2)}) async-start(), calls=%async_computation.2 | async-start | bytes 3784704 | tf_op jit(solution)/shard_map/reduce_scatter | solution.py:174
  12.7 19.7 %collective-permute-start = (bf16[3]{0:T(256)(128)(2,1)S(1)}, bf16[3]{0:T(256)(128)(2,1)S(1)}, u32[]{:S(2)}, u32[]{:S(2)}) collective-permute-start(bf16[3]{0:T(256)(128)(2,1)S(1)} %slice.118), channel_id=1, source_target_pairs={{0,32},{32,64},{64,96},{96,128},{128,160},{160,192},{192,224},{1,3... | collective-permute-start | bytes 26 | tf_op jit(solution)/shard_map/ppermute | solution.py:14
  96.1 5.7 %copy-start.2 = (bf16[3584,128]{1,0:T(8,128)(2,1)S(1)}, bf16[3584,128]{1,0:T(8,128)(2,1)}, u32[]{:S(2)}) copy-start(bf16[3584,128]{1,0:T(8,128)(2,1)} %param.18) | copy-start | bytes 2752516
  96.2 5.6 %copy-start.1 = (bf16[512,3584]{0,1:T(8,128)(2,1)S(1)}, bf16[512,3584]{0,1:T(8,128)(2,1)}, u32[]{:S(2)}) copy-start(bf16[512,3584]{0,1:T(8,128)(2,1)} %all-gather.6.cloned.1.call-done) | copy-start | bytes 11010052
  99.9 16.4 %collective-permute-start.1 = (bf16[3,128]{1,0:T(4,128)(2,1)S(1)}, bf16[3,128]{1,0:T(4,128)(2,1)S(1)}, u32[]{:S(2)}, u32[]{:S(2)}) collective-permute-start(bf16[3,128]{1,0:T(4,128)(2,1)S(1)} %slice.152), channel_id=1, source_target_pairs={{0,32},{32,64},{64,96},{96,128},{128,160},{160,192},{192,224},{1,3... | collective-permute-start | bytes 2312 | tf_op jit(solution)/shard_map/ppermute | solution.py:14
  103.0 14.3 %collective-permute-start.2 = (bf16[3,128]{1,0:T(4,128)(2,1)S(1)}, bf16[3,128]{1,0:T(4,128)(2,1)S(1)}, u32[]{:S(2)}, u32[]{:S(2)}) collective-permute-start(bf16[3,128]{1,0:T(4,128)(2,1)S(1)} %slice.157), channel_id=1, source_target_pairs={{0,32},{32,64},{64,96},{96,128},{128,160},{160,192},{192,224},{1,3... | collective-permute-start | bytes 2312 | tf_op jit(solution)/shard_map/ppermute | solution.py:14
  117.9 35.0 %copy-start.3 = (s32[512]{0:T(512)S(1)}, s32[512]{0:T(512)}, u32[]{:S(2)}) copy-start(s32[512]{0:T(512)} %param.27) | copy-start | bytes 6148
  117.9 35.0 %copy-start.5 = (f32[2]{0:T(128)S(1)}, f32[2]{0:T(128)}, u32[]{:S(2)}) copy-start(f32[2]{0:T(128)} %param.22) | copy-start | bytes 28
  153.5 75.6 %copy-start.4 = (f32[128]{0:T(128)S(1)}, f32[128]{0:T(128)}, u32[]{:S(2)}) copy-start(f32[128]{0:T(128)} %param.25) | copy-start | bytes 1540
Sparse Core Ops, SparseCore 0:
  9.9 83.4 all-gather.5
  232.2 232.0 reduce-scatter.1
where the time goes:
time: 472 us; the launch traced here: 471 us
  waiting for transfers between devices  292 us (62%)
  blocking collectives  104 us (22%)
  local copies, waits for them, and re-layouts  18.2 us (4%)
  matrix products  17.9 us (4%)
  between operations  15 us (3%)
  other arithmetic  8.35 us (2%)
  loops' own time  7.88 us (2%)
  starting transfers between devices  7.37 us (2%)
    reduce_scatter x1, waiting for transfers between devices, local(): lax.psum_scatter(jnp.dot(normed, w_out, preferred_element_type=jnp.float3...  232 us
    psum x1, blocking collectives, local(): total_squares = lax.psum(local_squares, 'tensor')  71.9 us
    all_gather x1, waiting for transfers between devices, local(): piece = lax.all_gather(tokens, 'tensor', axis=1, tiled=True)  59.5 us
    all_gather x2, blocking collectives, entering(): lax.all_gather(a.astype(kind), axis)  20 us
    unnamed x1, blocking collectives  12 us
  transfers between devices with their start and end apart: 5, of which 2 were waited for; matrix products, arithmetic and copies ran while one was open for 3% of the time, Pallas kernels for 0%

commit v1 on v0

--- a/solution.py
+++ b/solution.py
@@ -99,7 +99,9 @@
     head_size = inner_w // heads
     state_w = w_bc.shape[1] // 2
     rim_len = conv_x.shape[0] - 1
-    piece = lax.all_gather(tokens, "tensor", axis=1, tiled=True)
+    piece = jnp.concatenate(
+        lax.all_to_all(jnp.stack([tokens] * lax.axis_size("tensor")), "tensor", 0, 0), axis=1
+    )
     gate_rows = w_zx[0]
     inner_rows = w_zx[1]
     gate_sum = jnp.dot(piece, gate_rows, preferred_element_type=jnp.float32)

time: 472 us -> 487 us (1.032)
  starting transfers between devices: 7.37 us -> 19 us
    all_to_all x0 -> x1, waiting for transfers between devices: none -> 62.6 us  [local(): lax.all_to_all(jnp.stack([tokens] * lax.axis_size('tensor')), 'tensor', 0...]
    all_gather x1 -> x0, waiting for transfers between devices: 59.5 us -> none  [local(): piece = lax.all_gather(tokens, 'tensor', axis=1, tiled=True)]
    all_to_all x0 -> x1, starting transfers between devices: none -> 11.6 us  [local(): lax.all_to_all(jnp.stack([tokens] * lax.axis_size('tensor')), 'tensor', 0...]
where the time goes in v1:
time: 487 us; the launch traced here: 486 us
  waiting for transfers between devices  296 us (61%)
  blocking collectives  104 us (21%)
  matrix products  19.6 us (4%)
  starting transfers between devices  19 us (4%)
  local copies, waits for them, and re-layouts  18 us (4%)
  between operations  15.1 us (3%)
  loops' own time  8.42 us (2%)
  other arithmetic  5.69 us (1%)
    reduce_scatter x1, waiting for transfers between devices, local(): lax.psum_scatter(jnp.dot(normed, w_out, preferred_element_type=jnp.float3...  233 us
    psum x1, blocking collectives, local(): total_squares = lax.psum(local_squares, 'tensor')  71.5 us
    all_to_all x1, waiting for transfers between devices, local(): lax.all_to_all(jnp.stack([tokens] * lax.axis_size('tensor')), 'tensor', 0...  62.6 us
    all_gather x2, blocking collectives, entering(): lax.all_gather(a.astype(kind), axis)  20.1 us
    unnamed x1, blocking collectives  12.5 us
    all_to_all x1, starting transfers between devices, local(): lax.all_to_all(jnp.stack([tokens] * lax.axis_size('tensor')), 'tensor', 0...  11.6 us
  transfers between devices with their start and end apart: 5, of which 2 were waited for; matrix products, arithmetic and copies ran while one was open for 3% of the time, Pallas kernels for 0%

profile of v1, /device:TPU:8, one launch (start us, length us, event | category | flops | bytes accessed | tf_op | source)
XLA Modules:
  0.0 485.8 jit_solution(11273821315211636196)
XLA Ops:
  6.5 3.2 stack.2
  9.8 11.6 %all-to-all-start = ((bf16[32,512,112]{1,2,0:T(8,128)(2,1)}), bf16[32,512,112]{1,2,0:T(8,128)(2,1)}, u32[]{:S(2)}, u32[]{:S(2)}) async-start(bf16[32,512,112]{1,2,0:T(8,128)(2,1)} %stack.2), calls=%async_computation | async-start | bytes 7340032 | tf_op jit(solution)/shard_map/all_to_all | solution.py:103
  22.7 1.4 dynamic-update-slice
  24.1 1.4 dynamic-update-slice.1
  25.5 1.9 collective-permute-start
  27.4 12.5 %all-reduce.2 = (bf16[8]{0:T(256)(128)(2,1)S(1)}, bf16[8]{0:T(256)(128)(2,1)S(1)}) all-reduce(bf16[8]{0:T(256)(128)(2,1)S(1)} %dynamic-update-slice, bf16[8]{0:T(256)(128)(2,1)S(1)} %dynamic-update-slice.1), channel_id=2, replica_groups=mesh['seq'=8,'tensor'=32] {'seq'}, use_global_device_ids=true, to_apply=%add | all-reduce | flops 16 | bytes 64
  40.0 0.7 fusion.81
  42.2 62.6 %all-to-all-done = bf16[32,512,112]{1,2,0:T(8,128)(2,1)} async-done(((bf16[32,512,112]{1,2,0:T(8,128)(2,1)}), bf16[32,512,112]{1,2,0:T(8,128)(2,1)}, u32[]{:S(2)}, u32[]{:S(2)}) %all-to-all-start) | async-done | bytes 3670048 | tf_op jit(solution)/shard_map/all_to_all | solution.py:103
  104.7 3.3 fusion.84
  108.1 1.9 collective-permute-start.2
  110.0 3.2 fusion.83
  113.2 3.6 collective-permute-start.1
  116.8 2.6 broadcast_multiply_fusion
  120.8 8.5 %all-gather.3 = bf16[8,1,2]{2,1,0:T(2,128)(2,1)S(1)} all-gather(bf16[1,1,2]{2,1,0:T(2,128)(2,1)S(1)} %bitcast.200), channel_id=1, replica_groups=mesh['seq'=8,'tensor'=32] {'seq'}, dimensions={0}, use_global_device_ids=true | all-gather | bytes 36 | tf_op jit(solution)/shard_map/all_gather | solution.py:20
  131.2 16.7 %while.31 = (s32[]{:T(128)}, f32[2,64,64]{2,1,0:T(8,128)S(1)}, s32[]{:T(128)}, f32[2,256,2,64]{1,0,3,2:T(2,128)S(1)}, s32[2,256]{1,0:T(2,128)S(1)}, /*index=5*/f...) while((s32[]{:T(128)}, f32[2,64,64]{2,1,0:T(8,128)S(1)}, ...), condition=%wide.region_3.4_spmd.clone, body=%wide.region_0.3_spmd.clone.sunk | while | flops 202246672 | bytes 2326370 | solution.py:151
  131.2 0.7 dynamic-slice.4
  131.9 0.7 broadcast_compare_fusion.3
  132.6 0.6 reduce-window.26
  135.0 0.8 fusion.114
  135.9 1.9 dynamic_update_slice.6
  139.5 0.7 dynamic-slice.4
  140.2 0.7 broadcast_compare_fusion.3
  143.3 0.8 fusion.114
  144.2 1.9 dynamic_update_slice.6
  147.9 11.6 %all-gather.1 = bf16[16,64,64]{2,1,0:T(8,128)(2,1)S(1)} all-gather(bf16[2,64,64]{2,1,0:T(8,128)(2,1)S(1)} %convert_element_type.85), channel_id=3, replica_groups=mesh['seq'=8,'tensor'=32] {'seq'}, dimensions={0}, use_global_device_ids=true | all-gather | bytes 147456 | tf_op jit(solution)/shard_map/all_gather | solution.py:20
  159.5 7.3 %while.30 = (s32[]{:T(128)}, f32[2,64,64]{2,1,0:T(8,128)S(1)}, f32[1]{0:T(128)}, s32[]{:T(128)}, bf16[8,1]{0,1:T(2,128)(2,1)S(1)}, /*index=5*/bf16[8,2]{0,1:T(2,...) while((s32[]{:T(128)}, f32[2,64,64]{2,1,0:T(8,128)S(1)}, ...), condition=%wide.region_7.8_spmd, body=%wide.region_6.7_spmd.sunk | while | flops 24592 | bytes 82175 | solution.py:36
  159.5 0.7 constant_dynamic-slice_fusion.7
  163.2 0.7 constant_dynamic-slice_fusion.7
  167.8 3.5 multiply_reduce_fusion
  171.3 71.5 %psum.7 = f32[512]{0:T(512)S(1)} all-reduce(f32[512]{0:T(512)S(1)} %get-tuple-element.290), channel_id=1, replica_groups=mesh['seq'=8,'tensor'=32] {'tensor'}, use_global_device_ids=true, to_apply=%region_9.10 | all-reduce | flops 512 | bytes 4096 | tf_op jit(solution)/shard_map/psum | solution.py:173
  242.8 3.0 convolution_convert_fusion
  245.8 233.2 %reduce-scatter.2.cloned.1.call-done = bf16[16,3584]{1,0:T(8,128)(2,1)} async-done(((bf16[512,3584]{1,0:T(8,128)(2,1)}), bf16[16,3584]{1,0:T(8,128)(2,1)}) %reduce-scatter.2.cloned.1.call-update) | async-done | bytes 114704 | tf_op jit(solution)/shard_map/reduce_scatter | solution.py:176
  (121 shorter events, 11.3 us)
Async XLA Ops:
  6.5 236.3 %copy-start = (bf16[128,3584]{1,0:T(8,128)(2,1)S(1)}, bf16[128,3584]{1,0:T(8,128)(2,1)}, u32[]{:S(2)}) copy-start(bf16[128,3584]{1,0:T(8,128)(2,1)} %param.26) | copy-start | bytes 2752516
  9.8 11.7 %copy-start.2 = (s32[512]{0:T(512)S(1)}, s32[512]{0:T(512)}, u32[]{:S(2)}) copy-start(s32[512]{0:T(512)} %param.27) | copy-start | bytes 6148
  9.8 11.8 %copy-start.11 = (u32[256]{0:T(256)S(1)}, u32[256]{0:T(256)}, u32[]{:S(2)}) copy-start(u32[256]{0:T(256)} %constant.90) | copy-start | bytes 3076
  9.8 30.2 %copy-start.9 = (f32[2]{0:T(128)S(1)}, f32[2]{0:T(128)}, u32[]{:S(2)}) copy-start(f32[2]{0:T(128)} %param.21) | copy-start | bytes 28
  9.8 32.2 %copy-start.4 = (f32[4,128]{1,0:T(4,128)S(1)}, f32[4,128]{1,0:T(4,128)}, u32[]{:S(2)}) copy-start(f32[4,128]{1,0:T(4,128)} %param.24) | copy-start | bytes 6148
  9.8 32.2 %copy-start.5 = (f32[4,128]{1,0:T(4,128)S(1)}, f32[4,128]{1,0:T(4,128)}, u32[]{:S(2)}) copy-start(f32[4,128]{1,0:T(4,128)} %param.23) | copy-start | bytes 6148
  9.8 94.9 %copy-start.1 = (bf16[3584,128]{1,0:T(8,128)(2,1)S(1)}, bf16[3584,128]{1,0:T(8,128)(2,1)}, u32[]{:S(2)}) copy-start(bf16[3584,128]{1,0:T(8,128)(2,1)} %param.18) | copy-start | bytes 2752516
  9.8 94.9 %all-to-all-start = ((bf16[32,512,112]{1,2,0:T(8,128)(2,1)}), bf16[32,512,112]{1,2,0:T(8,128)(2,1)}, u32[]{:S(2)}, u32[]{:S(2)}) async-start(bf16[32,512,112]{1,2,0:T(8,128)(2,1)} %stack.2), calls=%async_computation | async-start | bytes 7340032 | tf_op jit(solution)/shard_map/all_to_all | solution.py:103
  21.4 457.6 %reduce-scatter.2.cloned.1.call-start = ((), (), s32[]{:S(2)}) async-start(), calls=%async_computation.2 | async-start | bytes 3784704 | tf_op jit(solution)/shard_map/reduce_scatter | solution.py:176
  25.5 16.5 %collective-permute-start = (bf16[3]{0:T(256)(128)(2,1)S(1)}, bf16[3]{0:T(256)(128)(2,1)S(1)}, u32[]{:S(2)}, u32[]{:S(2)}) collective-permute-start(bf16[3]{0:T(256)(128)(2,1)S(1)} %slice.118), channel_id=1, source_target_pairs={{0,32},{32,64},{64,96},{96,128},{128,160},{160,192},{192,224},{1,3... | collective-permute-start | bytes 26 | tf_op jit(solution)/shard_map/ppermute | solution.py:14
  104.7 5.3 %copy-start.7 = (bf16[2,3584,128]{2,1,0:T(8,128)(2,1)S(1)}, bf16[2,3584,128]{2,1,0:T(8,128)(2,1)}, u32[]{:S(2)}) copy-start(bf16[2,3584,128]{2,1,0:T(8,128)(2,1)} %param.17) | copy-start | bytes 5505028
  108.1 8.8 %copy-start.8 = (bf16[3584,2]{0,1:T(2,128)(2,1)S(1)}, bf16[3584,2]{0,1:T(2,128)(2,1)}, u32[]{:S(2)}) copy-start(bf16[3584,2]{0,1:T(2,128)(2,1)} %param.19) | copy-start | bytes 43012
  108.1 8.8 %copy-start.10 = (f32[2]{0:T(128)S(1)}, f32[2]{0:T(128)}, u32[]{:S(2)}) copy-start(f32[2]{0:T(128)} %param.20) | copy-start | bytes 28
  108.1 22.2 %collective-permute-start.2 = (bf16[3,128]{1,0:T(4,128)(2,1)S(1)}, bf16[3,128]{1,0:T(4,128)(2,1)S(1)}, u32[]{:S(2)}, u32[]{:S(2)}) collective-permute-start(bf16[3,128]{1,0:T(4,128)(2,1)S(1)} %slice.157), channel_id=1, source_target_pairs={{0,32},{32,64},{64,96},{96,128},{128,160},{160,192},{192,224},{1,3... | collective-permute-start | bytes 2312 | tf_op jit(solution)/shard_map/ppermute | solution.py:14
  113.2 16.3 %collective-permute-start.1 = (bf16[3,128]{1,0:T(4,128)(2,1)S(1)}, bf16[3,128]{1,0:T(4,128)(2,1)S(1)}, u32[]{:S(2)}, u32[]{:S(2)}) collective-permute-start(bf16[3,128]{1,0:T(4,128)(2,1)S(1)} %slice.152), channel_id=1, source_target_pairs={{0,32},{32,64},{64,96},{96,128},{128,160},{160,192},{192,224},{1,3... | collective-permute-start | bytes 2312 | tf_op jit(solution)/shard_map/ppermute | solution.py:14
  131.2 35.9 %copy-start.6 = (f32[2]{0:T(128)S(1)}, f32[2]{0:T(128)}, u32[]{:S(2)}) copy-start(f32[2]{0:T(128)} %param.22) | copy-start | bytes 28
  167.6 75.2 %copy-start.3 = (f32[128]{0:T(128)S(1)}, f32[128]{0:T(128)}, u32[]{:S(2)}) copy-start(f32[128]{0:T(128)} %param.25) | copy-start | bytes 1540
Sparse Core Ops, SparseCore 0:
  245.9 233.0 reduce-scatter.1
